TPU v7x, 256 devices: a whole 4x4x8 slice. The times are simulated.
256 devices in a mesh: ref: 64 (over z, y_lo, x), win: 4 (over y_hi, core).
Axes of the slice: x: 4, y: 4 (y_hi: 2, y_lo: 2; y = y_hi * 2 + y_lo), z: 8, core: 2. Of those that a mesh axis runs over, the one named last changes fastest.
Arguments:
- queries: bfloat16 [2048, 8192], P('ref', 'win'), may hold values from -1 to 1, as said below
- references: bfloat16 [65536, 8192], P('ref', 'win'), may hold values from -1 to 1, as said below
- labels: int32 [512], P('ref'), may hold values from 0 to 7, as said below
- kernel: float32 [9, 8], replicated, may hold values from 0.02 to 0.3
- class_bias: float32 [8], replicated, may hold values from -4 to 4
Outputs:
- ancestry_logprob: float32 [16, 8, 2048], P('win', None, 'ref')
Inputs may be any that keep to these rules, and one draw needn't show every extreme that they name: `queries`: every entry is -1 or +1. `references`: every entry is -1 or +1. Every ancestry labels at least one block.
All inputs are finite; a program needn't handle non-finite values.
Results may differ from a plain program's by a relative error of at most 0.0003.
Values may be sent and summed in bfloat16 or wider, within the bound.
A program may use at most 64 MiB of HBM per device.

v0:
```python
import jax
import jax.numpy as jnp
from jax import lax
from jax.sharding import PartitionSpec as P

S = 512
A = 8
BLOCK = 128
TAPS = 9


neg_floor = -1e30


def combined_all(shard, axis, combine):
    everything = lax.all_gather(shard, axis)
    leading = everything[0]

    def lap(k, so_far):
        return combine(so_far, everything[k])

    return lax.fori_loop(1, lax.axis_size(axis), lap, leading)


def with_halo(block, sides, width):
    for axis, dim in sides:
        count = lax.axis_size(axis)
        forward = [(i, i + 1) for i in range(count - 1)]
        backward = [(target, source) for source, target in forward]
        low = lax.ppermute(
            lax.slice_in_dim(block, block.shape[dim] - width, None, axis=dim), axis, forward
        )
        high = lax.ppermute(lax.slice_in_dim(block, 0, width, axis=dim), axis, backward)
        block = jnp.concatenate([low, block, high], axis=dim)
    return block


def pool_rows(query_piece, references, member, windows):
    score_scale = 256.0 / S
    row_count = query_piece.shape[0]
    block_count = references.shape[0] // BLOCK
    results = []
    for window in range(windows):
        query_part = query_piece[:, window * S : (window + 1) * S]
        ref_part = references[:, window * S : (window + 1) * S]
        scores = (
            jnp.einsum("qs,rs->qr", query_part, ref_part, preferred_element_type=jnp.float32)
            * score_scale
        )
        blocks = scores.reshape(row_count, block_count, BLOCK)
        block_peak = jnp.max(blocks, axis=2)
        block_total = jnp.sum(jnp.exp(blocks - block_peak[:, :, None]), axis=2)
        group_peak = jnp.max(jnp.where(member[None], block_peak[:, :, None], neg_floor), axis=1)
        weights = jnp.where(
            member[None],
            block_total[:, :, None] * jnp.exp(block_peak[:, :, None] - group_peak[:, None, :]),
            0.0,
        )
        group_total = jnp.sum(weights, axis=1)
        group_lse = jnp.where(group_total > 0, group_peak + jnp.log(group_total), neg_floor)
        results.append(group_lse.T)
    return jnp.stack(results)


def combine_lse(left_part, right_part):
    higher = jnp.maximum(left_part, right_part)
    return higher + jnp.log(jnp.exp(left_part - higher) + jnp.exp(right_part - higher))


def per_device(queries, references, labels, kernel, class_bias):
    member = labels[:, None] == jnp.arange(A, dtype=jnp.int32)[None, :]
    windows = references.shape[1] // S
    query_count = queries.shape[0]
    partial_value = pool_rows(
        lax.all_gather(queries, "ref", axis=0, tiled=True), references, member, windows
    )
    owner_start = lax.axis_index("ref") * query_count
    combined = combined_all(partial_value, "ref", combine_lse)
    pooled = lax.dynamic_slice_in_dim(combined, owner_start, query_count, 2)
    centered = pooled - jnp.mean(pooled, axis=1, keepdims=True)
    padded = with_halo(centered, (("win", 0),), TAPS // 2)
    smoothed = jnp.zeros_like(centered)
    for offset in range(TAPS):
        smoothed = smoothed + kernel[offset][None, :, None] * padded[offset : offset + windows]
    logits = smoothed + class_bias[None, :, None]
    return jax.nn.log_softmax(logits, axis=1)


def solution(mesh):
    in_specs = (P("ref", "win"), P("ref", "win"), P("ref"), P(), P())
    out_specs = P("win", None, "ref")
    return jax.shard_map(
        per_device, mesh=mesh, in_specs=in_specs, out_specs=out_specs, check_vma=False
    )
```

profile of v0, /device:TPU:1, one launch (start us, length us, event | category | flops | bytes accessed | tf_op | source)
XLA Modules:
  0.0 761.7 jit_solution(14383319232930999667)
XLA Ops:
  8.0 274.8 %all-gather.4.cloned.1.call-done = bf16[2048,2048]{1,0:T(8,128)(2,1)} async-done(((bf16[32,2048]{1,0:T(8,128)(2,1)}), bf16[2048,2048]{1,0:T(8,128)(2,1)}) %all-gather.4.cloned.1.call-update) | async-done | bytes 8388624 | tf_op jit(solution)/shard_map/all_gather | solution.py:75
  282.9 4.4 bitcast_reduce_fusion.3
  287.3 1.5 fusion.15
  288.9 1.8 copy-done.1
  290.7 2.4 bitcast_reduce_fusion
  293.1 1.5 fusion.9
  294.6 2.4 bitcast_reduce_fusion.1
  297.0 1.5 fusion.11
  298.5 2.6 bitcast_reduce_fusion.2
  301.1 1.5 fusion.13
  304.1 325.6 %all-gather.6.cloned.1.call-done = f32[256,8,2048]{2,1,0:T(8,128)} async-done(((f32[4,8,2048]{2,1,0:T(8,128)}), f32[256,8,2048]{2,1,0:T(8,128)}) %all-gather.6.cloned.1.call-update) | async-done | bytes 16777232 | tf_op jit(solution)/shard_map/all_gather | solution.py:16
  630.6 76.0 %while.15 = (s32[]{:T(128)}, f32[4,8,2048]{2,1,0:T(8,128)S(1)}, f32[64,4,8,2048]{3,2,1,0:T(8,128)}, s32[]{:T(128)}, s32[]{:T(128)}, /*index=5*/s32[]{:T(128)}) while((s32[]{:T(128)}, f32[4,8,2048]{2,1,0:T(8,128)S(1)}, f32[64,4,8,2048]{3,2,1,0:T(8,128)}, s32[]{:T(128)}, s32[]{:T(128)}, /*index=5*/s32[]{:T(128)}) %tuple.62), condition=%wide.region_17.18_spmd, body=%wide.region_16.17_spmd.sunk | while | flops 327685 | bytes 786539 | solution.py:22
  631.8 1.2 fusion.53
  634.2 1.2 fusion.53
  636.6 1.2 fusion.53
  639.0 1.2 fusion.53
  641.4 1.2 fusion.53
  643.9 1.2 fusion.53
  646.3 1.2 fusion.53
  648.7 1.2 fusion.53
  652.3 1.2 fusion.53
  654.7 1.2 fusion.53
  706.7 42.3 %collective-permute-start.1 = (f32[4,8,32]{2,1,0:T(8,128)S(1)}, f32[4,8,32]{2,1,0:T(8,128)S(1)}, u32[]{:S(2)}, u32[]{:S(2)}) collective-permute-start(f32[4,8,32]{2,1,0:T(8,128)S(1)} %dynamic-slice_subtract_fusion), channel_id=1, source_target_pairs={{1,0},{2,1},{3,2},{5,4},{6,5},{7,6},{9,8},{10,9},{11,10},{13,12},{... | collective-permute-start | bytes 12296 | tf_op jit(solution)/shard_map/ppermute | solution.py:33
  749.0 4.3 collective-permute-start
  (80 shorter events, 68.6 us)
Async XLA Ops:
  6.5 276.3 %all-gather.4.cloned.1.call-start = ((), (), s32[]{:S(2)}) async-start(), calls=%async_computation | async-start | bytes 8519680 | tf_op jit(solution)/shard_map/all_gather | solution.py:75
  7.3 622.4 %all-gather.6.cloned.1.call-start = ((), (), s32[]{:S(2)}) async-start(), calls=%async_computation.1 | async-start | bytes 17039360 | tf_op jit(solution)/shard_map/all_gather | solution.py:16
  282.9 6.0 copy-start.2
  287.3 3.4 copy-start.1
  301.1 452.2 %copy-start = (f32[9,8]{0,1:T(8,128)S(1)}, f32[9,8]{0,1:T(8,128)}, u32[]{:S(2)}) copy-start(f32[9,8]{0,1:T(8,128)} %param.10) | copy-start | bytes 868
  301.1 453.1 %copy-start.3 = (f32[8]{0:T(128)S(1)}, f32[8]{0:T(128)}, u32[]{:S(2)}) copy-start(f32[8]{0:T(128)} %param.11) | copy-start | bytes 100
  706.7 46.9 %collective-permute-start.1 = (f32[4,8,32]{2,1,0:T(8,128)S(1)}, f32[4,8,32]{2,1,0:T(8,128)S(1)}, u32[]{:S(2)}, u32[]{:S(2)}) collective-permute-start(f32[4,8,32]{2,1,0:T(8,128)S(1)} %dynamic-slice_subtract_fusion), channel_id=1, source_target_pairs={{1,0},{2,1},{3,2},{5,4},{6,5},{7,6},{9,8},{10,9},{11,10},{13,12},{... | collective-permute-start | bytes 12296 | tf_op jit(solution)/shard_map/ppermute | solution.py:33
  749.0 5.2 collective-permute-start
Sparse Core Ops, SparseCore 0:
  9.1 273.7 all-gather.3
  304.2 325.3 all-gather.5
where the time goes:
time: 764 us; the launch traced here: 762 us
  waiting for transfers between devices  602 us (79%)
  other arithmetic  83.8 us (11%)
  starting transfers between devices  46.6 us (6%)
  between operations  13.6 us (2%)
  matrix products  11.8 us (2%)
    all_gather x1, waiting for transfers between devices, combined_all(): everything = lax.all_gather(shard, axis)  326 us
    all_gather x1, waiting for transfers between devices, per_device(): lax.all_gather(queries, 'ref', axis=0, tiled=True)  275 us
    add x63, other arithmetic, combine_lse(): higher + jnp.log(jnp.exp(left_part - higher) + jnp.exp(right_part - higher))  74.7 us
    ppermute x1, starting transfers between devices, with_halo(): lax.ppermute(lax.slice_in_dim(block, 0, width, axis=dim), axis, backward)  42.3 us
  transfers between devices with their start and end apart: 4, of which 3 were waited for; matrix products, arithmetic and copies ran while one was open for 0% of the time, Pallas kernels for 0%

commit v1 on v0

v1 whole, which is shorter than its diff:
```python
import math

import jax
import jax.numpy as jnp
from jax import lax
from jax.experimental import pallas as pl
from jax.experimental.pallas import tpu as pltpu
from jax.sharding import PartitionSpec as P

S = 512
A = 8
BLOCK = 128
TAPS = 9

Z, Y, X = 8, 2, 4
PEERS = Z * Y * X
WINDOWS = 4
ROWS = 32
REFS = 1024
BLOCKS = REFS // BLOCK
GROUP = 8
LANES = GROUP * ROWS
GROUPS = PEERS // GROUP
STEPS = GROUPS * WINDOWS

DIRECTIONS = ((1, 0, 0), (-1, 0, 0), (0, 0, 1), (0, 0, -1), (0, 1, 0))

SCHEDULE = (
    (64, 128, 192, 0, 128),
    (0, 0, 64, 128, 0),
    (192, 192, 128, 192, 64),
    (128, 64, 0, 64, 192),
    (72, 184, 72, 3, 3),
    (193, 56, 193, 132, 72),
    (132, 248, 65, 131, 193),
    (8, 120, 132, 68, 8),
    (200, 193, 8, 196, 200),
    (129, 65, 68, 248, 1),
    (136, 129, 56, 120, 56),
    (80, 131, 176, 56, 248),
    (7, 132, 48, 80, 120),
    (135, 240, 240, 76, 48),
    (16, 48, 112, 204, 240),
    (208, 176, 201, 208, 176),
    (144, 112, 9, 16, 112),
    (66, 251, 137, 144, 208),
    (12, 187, 177, 48, 80),
    (140, 123, 49, 15, 88),
    (83, 241, 241, 143, 24),
    (88, 177, 113, 79, 202),
    (216, 49, 104, 216, 216),
    (152, 40, 152, 24, 152),
    (147, 243, 88, 211, 40),
    (10, 180, 24, 40, 178),
    (138, 116, 216, 104, 232),
    (74, 179, 212, 91, 50),
    (14, 114, 148, 28, 242),
    (78, 178, 84, 220, 114),
    (206, 242, 20, 156, 91),
    (142, 50, 153, 219, 235),
    (18, 182, 172, 172, 43),
    (182, 54, 236, 108, 105),
    (54, 246, 44, 96, 106),
    (246, 235, 32, 32, 90),
    (118, 169, 96, 160, 160),
    (214, 44, 224, 159, 96),
    (220, 239, 28, 31, 153),
    (213, 174, 92, 124, 121),
    (95, 46, 190, 252, 249),
    (94, 238, 60, 190, 59),
    (154, 47, 33, 99, 163),
    (239, 234, 180, 180, 33),
    (45, 237, 100, 52, 115),
    (237, 95, 164, 118, 147),
    (207, 25, 140, 20, 85),
    (69, 217, 204, 14, 149),
    (254, 2, 121, 7, 190),
    (126, 83, 10, 251, 130),
    (195, -1, -1, 136, -1),
)

RESIDENCE = 3
SLOT_US = 0.70
STEP_US = 0.65
ISSUE_AHEAD_US = 1.4
ARRIVAL_US = 1.9

LOG2_E = math.log2(math.e)
SCALE = 256.0 / S
NEG_FLOOR = -1e30
MESH = pl.DeviceIdType.MESH


def moved(offset, step):
    z, y, x = offset // (Y * X), offset // X % Y, offset % X
    return ((z + step[0]) % Z * Y + (y + step[1]) % Y) * X + (x + step[2]) % X


def make_plan():
    arrival = {}
    for time, row in enumerate(SCHEDULE):
        for step, piece in zip(DIRECTIONS, row):
            if piece >= 0:
                window, offset = divmod(piece, PEERS)
                arrival[window, moved(offset, step)] = time
    assert len(arrival) == WINDOWS * (PEERS - 1)
    rank = {
        offset: (
            max(arrival[w, offset] for w in range(WINDOWS)),
            sum(arrival[w, offset] for w in range(WINDOWS)),
            offset,
        )
        for offset in range(1, PEERS)
    }
    order = [0] + sorted(rank, key=rank.get)
    ready = []
    for step in range(STEPS):
        group, window = divmod(step, WINDOWS)
        members = order[group * GROUP : (group + 1) * GROUP]
        last = max(arrival[window, o] for o in members if o)
        ready.append((last + 1) * SLOT_US + ARRIVAL_US)
    before = []
    now, time = 0.0, 0
    for step in range(STEPS):
        sends = []
        while True:
            due = time * SLOT_US - ISSUE_AHEAD_US if time < len(SCHEDULE) else 1e9
            if due <= now or due <= ready[step]:
                if due > now and ready[step] <= now:
                    break
                now = max(now, due)
                sends.append(time)
                time += 1
                continue
            break
        now = max(now, ready[step]) + STEP_US
        before.append(sends)
    before.append(list(range(time, len(SCHEDULE))))
    return order, before


def kernel_body(
    queries, references, labels, taps, bias, out,
    qbuf, rbuf, scores, pooled_part, result, inbox, halo, centred,
    own_sem, ref_sem, send_sem, recv_sem, result_send, result_recv,
    halo_send, halo_recv,
):
    order, before = make_plan()
    slot_of = {offset: slot for slot, offset in enumerate(order)}

    me = lax.axis_index("ref")
    win = lax.axis_index("win")
    mz, my, mx = me // (Y * X), me // X % Y, me % X

    def peer(step):
        z = lax.rem(mz + (step[0] + Z), Z)
        y = lax.rem(my + (step[1] + Y), Y)
        x = lax.rem(mx + (step[2] + X), X)
        return (z * Y + y) * X + x

    neighbours = [peer(step) for step in DIRECTIONS]
    sides = [lax.rem(win + 3, 4), lax.rem(win + 1, 4)]

    def own_copy(window):
        return pltpu.make_async_copy(
            queries.at[:, pl.ds(window * S, S)],
            qbuf.at[window, pl.ds(0, ROWS), :],
            own_sem.at[window],
        )

    def ref_copy(window):
        return pltpu.make_async_copy(
            references.at[:, pl.ds(window * S, S)], rbuf.at[window], ref_sem.at[window]
        )

    def piece_ref(window, offset):
        return qbuf.at[window, pl.ds(slot_of[offset] * ROWS, ROWS), :]

    def piece_copy(window, offset, direction):
        landing = moved(offset, DIRECTIONS[direction])
        return pltpu.make_async_remote_copy(
            src_ref=piece_ref(window, offset),
            dst_ref=piece_ref(window, landing),
            send_sem=send_sem.at[direction],
            recv_sem=recv_sem.at[window, slot_of[landing]],
            device_id={"ref": neighbours[direction]},
            device_id_type=MESH,
        )

    def arrived(window, offset):
        ref = piece_ref(window, offset)
        pltpu.make_async_remote_copy(
            src_ref=ref,
            dst_ref=ref,
            send_sem=send_sem.at[0],
            recv_sem=recv_sem.at[window, slot_of[offset]],
            device_id={"ref": neighbours[0]},
            device_id_type=MESH,
        ).wait_recv()

    def result_copy(slot):
        offset = order[slot]
        z, y, x = offset // (Y * X), offset // X % Y, offset % X
        return pltpu.make_async_remote_copy(
            src_ref=result.at[slot],
            dst_ref=inbox.at[slot],
            send_sem=result_send,
            recv_sem=result_recv,
            device_id={"ref": peer((-z, -y, -x))},
            device_id_type=MESH,
        )

    def halo_copy(side):
        return pltpu.make_async_remote_copy(
            src_ref=centred,
            dst_ref=halo.at[side],
            send_sem=halo_send.at[side],
            recv_sem=halo_recv.at[side],
            device_id={"win": sides[side]},
            device_id_type=MESH,
        )

    for window in range(WINDOWS):
        own_copy(window).start()
    barrier = pltpu.get_barrier_semaphore()
    for neighbour in neighbours:
        pl.semaphore_signal(
            barrier, inc=1, device_id={"ref": neighbour}, device_id_type=MESH
        )
    for side in sides:
        pl.semaphore_signal(barrier, inc=1, device_id={"win": side}, device_id_type=MESH)
    for window in range(WINDOWS):
        ref_copy(window).start()
    for window in range(WINDOWS):
        own_copy(window).wait()
    pl.semaphore_wait(barrier, len(neighbours) + len(sides))

    waited = {(window, 0) for window in range(WINDOWS)}

    def need(actions, window, offset):
        if (window, offset) not in waited:
            waited.add((window, offset))
            actions.append(("arrived", window, offset))

    def sends(actions, times):
        for time in times:
            for direction, piece in enumerate(SCHEDULE[time]):
                if piece >= 0:
                    window, offset = divmod(piece, PEERS)
                    need(actions, window, offset)
                    actions.append(("send", window, offset, direction))

    program = []
    for step in range(STEPS):
        group, window = divmod(step, WINDOWS)
        actions = []
        sends(actions, before[step])
        if step >= WINDOWS and window == 1:
            for slot in range((group - 1) * GROUP, group * GROUP):
                if slot:
                    actions.append(("result", slot))
        if group == 0:
            actions.append(("refs", window))
        for offset in order[group * GROUP : (group + 1) * GROUP]:
            need(actions, window, offset)
        program.append(actions)
    last = []
    sends(last, before[STEPS])
    for slot in range((GROUPS - 1) * GROUP, GROUPS * GROUP):
        last.append(("result", slot))

    def run(actions):
        for kind, *rest in actions:
            if kind == "arrived":
                arrived(*rest)
            elif kind == "send":
                piece_copy(*rest).start()
            elif kind == "result":
                result_copy(*rest).start()
            else:
                ref_copy(*rest).wait()

    row_of = lax.broadcasted_iota(jnp.int32, (A, LANES), 0)
    lane_window = lax.broadcasted_iota(jnp.int32, (A, 128), 1) // ROWS

    def select_actions(step, low, high):
        if high - low == 1:
            run(program[low])
            return
        middle = (low + high) // 2

        @pl.when(step < middle)
        def _():
            select_actions(step, low, middle)

        @pl.when(step >= middle)
        def _():
            select_actions(step, middle, high)

    def pool(group, window):
        query = qbuf[window, pl.ds(pl.multiple_of(group * LANES, LANES), LANES), :]
        scores[...] = lax.dot_general(
            rbuf[window], query, (((1,), (1,)), ((), ())),
            preferred_element_type=jnp.float32,
        )
        peaks, totals = [], []
        for block in range(BLOCKS):
            part = scores[block * BLOCK : (block + 1) * BLOCK, :]
            peak = jnp.max(part, axis=0, keepdims=True)
            peaks.append(peak)
            totals.append(
                jnp.sum(
                    jnp.exp2((part - peak) * (SCALE * LOG2_E)), axis=0, keepdims=True
                )
            )
        member = [row_of == labels[block] for block in range(BLOCKS)]
        group_peak = jnp.full((A, LANES), NEG_FLOOR, jnp.float32)
        for block in range(BLOCKS):
            group_peak = jnp.maximum(
                group_peak, jnp.where(member[block], peaks[block], NEG_FLOOR)
            )
        group_total = jnp.zeros((A, LANES), jnp.float32)
        for block in range(BLOCKS):
            power = jnp.where(
                member[block], (peaks[block] - group_peak) * (SCALE * LOG2_E), NEG_FLOOR
            )
            group_total = group_total + totals[block] * jnp.exp2(power)
        pooled_part[window] = jnp.where(
            group_total > 0, group_peak * SCALE + jnp.log(group_total), NEG_FLOOR
        )

    def collect(group):
        for member in range(GROUP):
            half, place = divmod(member, 128 // ROWS)
            tile = jnp.zeros((A, 128), jnp.float32)
            for window in range(WINDOWS):
                value = pooled_part[window, :, half * 128 : (half + 1) * 128]
                shift = (window - place) * ROWS % 128
                if shift:
                    value = pltpu.roll(value, shift, 1)
                tile = jnp.where(lane_window == window, value, tile)
            result[group * GROUP + member] = tile

    def body(step, carry):
        group, window = step // WINDOWS, step % WINDOWS
        select_actions(step, 0, STEPS)
        pool(group, window)

        @pl.when(window == WINDOWS - 1)
        def _():
            collect(group)

        return carry

    lax.fori_loop(0, STEPS, body, 0)
    run(last)

    pltpu.make_async_remote_copy(
        src_ref=inbox.at[pl.ds(1, PEERS - 1)],
        dst_ref=inbox.at[pl.ds(1, PEERS - 1)],
        send_sem=result_send,
        recv_sem=result_recv,
        device_id={"ref": neighbours[0]},
        device_id_type=MESH,
    ).wait_recv()
    inbox[0] = result[0]
    gathered = inbox[...]
    peak = jnp.max(gathered, axis=0)
    pooled = peak + jnp.log(jnp.sum(jnp.exp(gathered - peak[None]), axis=0))
    own = pooled - jnp.mean(pooled, axis=0, keepdims=True)
    centred[...] = own
    for side in range(2):
        halo_copy(side).start()

    row = row_of[:, :128]

    def column(read):
        tile = jnp.zeros((A, 128), jnp.float32)
        for ancestry in range(A):
            tile = jnp.where(row == ancestry, read(ancestry), tile)
        return tile

    weights = [column(lambda a, t=tap: taps[t, a]) for tap in range(TAPS)]
    offset_tile = column(lambda a: bias[a])

    for side in range(2):
        halo_copy(side).wait_recv()
    upper = jnp.where(win < 3, halo[0], 0.0)
    lower = jnp.where(win > 0, halo[1], 0.0)
    smoothed = jnp.zeros((A, 128), jnp.float32)
    for tap in range(TAPS):
        shift = tap - TAPS // 2
        if shift == 0:
            value = own
        elif abs(shift) == WINDOWS:
            value = upper if shift > 0 else lower
        else:
            amount = -shift * ROWS % 128
            inside = (lane_window + shift >= 0) & (lane_window + shift < WINDOWS)
            value = jnp.where(
                inside,
                pltpu.roll(own, amount, 1),
                pltpu.roll(upper if shift > 0 else lower, amount, 1),
            )
        smoothed = smoothed + weights[tap] * value
    logits = smoothed + offset_tile
    shifted = logits - jnp.max(logits, axis=0, keepdims=True)
    final = shifted - jnp.log(jnp.sum(jnp.exp(shifted), axis=0, keepdims=True))
    for window in range(WINDOWS):
        out[window] = final[:, window * ROWS : (window + 1) * ROWS]

    for direction in range(len(DIRECTIONS)):
        count = sum(row[direction] >= 0 for row in SCHEDULE)
        sent = qbuf.at[0, pl.ds(0, count * ROWS), :]
        pltpu.make_async_remote_copy(
            src_ref=sent,
            dst_ref=sent,
            send_sem=send_sem.at[direction],
            recv_sem=recv_sem.at[0, 0],
            device_id={"ref": neighbours[direction]},
            device_id_type=MESH,
        ).wait_send()
    pltpu.make_async_remote_copy(
        src_ref=result.at[pl.ds(1, PEERS - 1)],
        dst_ref=result.at[pl.ds(1, PEERS - 1)],
        send_sem=result_send,
        recv_sem=result_recv,
        device_id={"ref": neighbours[0]},
        device_id_type=MESH,
    ).wait_send()
    for side in range(2):
        halo_copy(side).wait_send()


def per_device(queries, references, labels, kernel, class_bias):
    hbm = pl.BlockSpec(memory_space=pl.ANY)
    smem = pl.BlockSpec(memory_space=pltpu.SMEM)
    return pl.pallas_call(
        kernel_body,
        out_shape=jax.ShapeDtypeStruct((WINDOWS, A, ROWS), jnp.float32),
        in_specs=[hbm, hbm, smem, smem, smem],
        out_specs=pl.BlockSpec(memory_space=pltpu.VMEM),
        scratch_shapes=[
            pltpu.VMEM((WINDOWS, PEERS * ROWS, S), jnp.bfloat16),
            pltpu.VMEM((WINDOWS, REFS, S), jnp.bfloat16),
            pltpu.VMEM((REFS, LANES), jnp.float32),
            pltpu.VMEM((WINDOWS, A, LANES), jnp.float32),
            pltpu.VMEM((PEERS, A, 128), jnp.float32),
            pltpu.VMEM((PEERS, A, 128), jnp.float32),
            pltpu.VMEM((2, A, 128), jnp.float32),
            pltpu.VMEM((A, 128), jnp.float32),
            pltpu.SemaphoreType.DMA((WINDOWS,)),
            pltpu.SemaphoreType.DMA((WINDOWS,)),
            pltpu.SemaphoreType.DMA((len(DIRECTIONS),)),
            pltpu.SemaphoreType.DMA((WINDOWS, PEERS)),
            pltpu.SemaphoreType.DMA,
            pltpu.SemaphoreType.DMA,
            pltpu.SemaphoreType.DMA((2,)),
            pltpu.SemaphoreType.DMA((2,)),
        ],
        compiler_params=pltpu.CompilerParams(collective_id=0, has_side_effects=True),
        name="ancestry",
    )(queries, references, labels, kernel, class_bias)


def solution(mesh):
    in_specs = (P("ref", "win"), P("ref", "win"), P("ref"), P(), P())
    out_specs = P("win", None, "ref")
    return jax.shard_map(
        per_device, mesh=mesh, in_specs=in_specs, out_specs=out_specs, check_vma=False
    )
```

time: 764 us -> 69 us (0.09)
  waiting for transfers between devices: 602 us -> 0 us
  other arithmetic: 83.8 us -> 0 us
  Pallas kernels: 0 us -> 66.1 us
  starting transfers between devices: 46.6 us -> 0 us
  between operations: 13.6 us -> 0.01 us
  matrix products: 11.8 us -> 0 us
    all_gather x2 -> x0, waiting for transfers between devices: 600 us -> none  [the longest x1 326 us: combined_all(): everything = lax.all_gather(shard, axis)]
    add x63 -> x0, other arithmetic: 74.7 us -> none  [combine_lse(): higher + jnp.log(jnp.exp(left_part - higher) + jnp.exp(right_part - higher))]
    pallas_call x0 -> x1, Pallas kernels: none -> 66.1 us  [per_device(): pl.pallas_call(kernel_body, out_shape=jax.ShapeDtypeStruct((WINDOWS, A, R...]
    ppermute x2 -> x0, starting transfers between devices: 46.6 us -> none  [the longest x1 42.3 us: with_halo(): lax.ppermute(lax.slice_in_dim(block, 0, width, axis=dim), axis, backward)]
    dot_general x4 -> x0, matrix products: 11.8 us -> none  [pool_rows(): jnp.einsum('qs,rs->qr', query_part, ref_part, preferred_element_type=jnp....]
  transfers between devices with their start and end apart: 4 -> 0, of which waited for: 3 -> 0; matrix products, arithmetic and copies ran while one was open for 0% -> 0% of each run, Pallas kernels for 0% -> 0%
where the time goes in v1:
time: 69 us; the launch traced here: 68.8 us
  Pallas kernels  66.1 us (96%)
  local copies, waits for them, and re-layouts  2.68 us (4%)
    pallas_call x1, Pallas kernels, per_device(): pl.pallas_call(kernel_body, out_shape=jax.ShapeDtypeStruct((WINDOWS, A, R...  66.1 us
    unnamed x2, local copies, waits for them, and re-layouts  2.68 us

profile of v1, /device:TPU:1, one launch (start us, length us, event | category | flops | bytes accessed | tf_op | source)
XLA Modules:
  0.0 68.8 jit_solution(15877484264114248210)
XLA Ops:
  0.0 1.4 %copy.6.taps = f32[9,8]{1,0:T(8,128)} copy(f32[9,8]{0,1:T(8,128)} %param.8) | data formatting | bytes 576 | tf_op args[3]
  1.4 66.1 %ancestry.1 = f32[4,8,32]{2,1,0:T(8,128)} custom-call(bf16[32,2048]{1,0:T(8,128)(2,1)} %queries.1, bf16[1024,2048]{1,0:T(8,128)(2,1)} %references.1, s32[8]{0:T(128)} %labels.1, f32[9,8]{1,0:T(8,128)} %copy.6.taps, f32[8]{0:T(128)} %bias.1), custom_call_target="tpu_custom_call" | custom-call | tf_op jit(solution)/shard_map/ancestry/pallas_call | solution.py:438
  67.4 1.3 %copy.8 = f32[4,8,32]{2,1,0:T(8,128)} copy(f32[4,8,32]{2,1,0:T(8,128)} %ancestry.1) | data formatting | bytes 8192
